TPU v7x, 32 devices: a whole 2x2x4 slice. The times are simulated.
32 devices in a mesh: mp: 2 (over x), width: 2 (over y), hidden: 8 (over z, core).
Axes of the slice: x: 2, y: 2, z: 4, core: 2. Of those that a mesh axis runs over, the one named last changes fastest.
Arguments:
- residual_in: bfloat16 [2, 512, 3584], P('mp', 'hidden'), may hold values from -6 to 6
- gate_weight: bfloat16 [2, 14336, 3584], P('mp', ('width', 'hidden')), may hold values from -0.09375 to 0.09375
- up_weight: bfloat16 [2, 14336, 3584], P('mp', ('width', 'hidden')), may hold values from -0.09375 to 0.09375
- down_weight: bfloat16 [2, 14336, 3584], P('mp', ('width', 'hidden')), may hold values from -0.046875 to 0.046875
- enc_weight: float32 [7168, 16384], P(('mp', 'width'), 'hidden'), may hold values from -0.0625 to 0.0625
- enc_bias: float32 [16384], P('hidden'), may hold values from -3 to 3
- dec_weight: float32 [16384, 7168], P('hidden', ('mp', 'width')), may hold values from -0.25 to 0.25
- dec_bias: float32 [7168], P(('mp', 'width')), may hold values from -2 to 2
Outputs:
- mlp_acts: bfloat16 [2, 512, 3584], P('mp', 'hidden', 'width')
- latents: float32 [512, 16384], P(None, 'hidden')
- grad_enc: float32 [7168, 16384], P(('mp', 'width'), 'hidden')
- grad_dec: float32 [16384, 7168], P('hidden', ('mp', 'width'))
- grad_enc_bias: float32 [16384], P('hidden')
- grad_dec_bias: float32 [7168], P(('mp', 'width'))
All inputs are finite; a program needn't handle non-finite values.
Results may differ from a plain program's by a relative error of at most 0.0058.
Values may be sent and summed in bfloat16 or wider, within the bound.
A program may use at most 192 MiB of HBM per device.

v0:
```python
import jax
import jax.numpy as jnp
from jax import lax
from jax.sharding import PartitionSpec as P

TOKENS = 512
sharpness = 8.0
sparsity_coef = 0.02
norm_floor = 1e-06
highest = lax.Precision.HIGHEST


def body(
    residual_in, gate_weight, up_weight, down_weight, enc_weight, enc_bias, dec_weight, dec_bias
):
    last_last = (((1,), (1,)), ((), ()))
    first_first = (((0,), (0,)), ((), ()))
    gathered = lax.all_gather(residual_in[0], "hidden", axis=0, tiled=True)
    gate_act = lax.dot_general(
        gathered, gate_weight[0], last_last, preferred_element_type=jnp.float32
    )
    up_act = lax.dot_general(gathered, up_weight[0], last_last, preferred_element_type=jnp.float32)
    hidden_act = (jax.nn.gelu(gate_act, approximate=True) * up_act).astype(jnp.bfloat16)
    down_local = down_weight[0]
    row_sums = lax.psum_scatter(
        jnp.dot(hidden_act, down_local, preferred_element_type=jnp.float32),
        "hidden",
        scatter_dimension=0,
        tiled=True,
    )
    model_sums = lax.psum_scatter(row_sums, "width", scatter_dimension=1, tiled=True)
    mlp_acts = model_sums.astype(jnp.bfloat16)
    coder_in = lax.all_gather(mlp_acts, "hidden", axis=0, tiled=True).astype(jnp.float32)
    enc_partial = jnp.dot(coder_in, enc_weight, precision=highest)
    model_index = lax.axis_index("mp")
    squares = jnp.sum(dec_weight * dec_weight, axis=1)
    square_pair = jnp.where(jnp.arange(2)[:, None] == model_index, squares[None, :], 0.0)
    pre_sum, square_sums = lax.psum((enc_partial, square_pair), ("mp", "width"))
    pre_act = pre_sum + enc_bias
    latents = jax.nn.softplus(sharpness * pre_act) / sharpness
    dec_norms = jnp.sqrt(square_sums + norm_floor)
    recon_part = jnp.dot(latents, dec_weight, precision=highest)
    own_rebuilt = lax.psum_scatter(recon_part, "hidden", scatter_dimension=0, tiled=True) + dec_bias
    own_grad = 2.0 / TOKENS * (own_rebuilt - mlp_acts.astype(jnp.float32))
    err_grad = lax.all_gather(own_grad.astype(jnp.bfloat16), "hidden", axis=0, tiled=True).astype(
        own_grad.dtype
    )
    grad_dec_bias = jnp.sum(err_grad, axis=0)
    back_part = lax.dot_general(
        err_grad, dec_weight, last_last, precision=highest, preferred_element_type=jnp.float32
    )
    lat_grad = lax.psum(back_part.astype(jnp.bfloat16), ("mp", "width")).astype(
        jnp.float32
    ) + sparsity_coef * (dec_norms[0] + dec_norms[1])
    pre_grad = lat_grad * jax.nn.sigmoid(sharpness * pre_act)
    grad_enc_bias = jnp.sum(pre_grad, axis=0)
    grad_enc = lax.dot_general(
        coder_in, pre_grad, first_first, precision=highest, preferred_element_type=jnp.float32
    )
    latent_totals = jnp.sum(latents, axis=0)
    own_norm = jnp.where(model_index == 0, dec_norms[0], dec_norms[1])
    grad_dec = lax.dot_general(
        latents, err_grad, first_first, precision=highest, preferred_element_type=jnp.float32
    )
    grad_dec = grad_dec + sparsity_coef * (latent_totals / own_norm)[:, None] * dec_weight
    return (mlp_acts[None], latents, grad_enc, grad_dec, grad_enc_bias, grad_dec_bias)


def solution(mesh):
    return jax.shard_map(
        body,
        mesh=mesh,
        in_specs=(
            P("mp", "hidden", None),
            P("mp", ("width", "hidden"), None),
            P("mp", ("width", "hidden"), None),
            P("mp", ("width", "hidden"), None),
            P(("mp", "width"), "hidden"),
            P("hidden"),
            P("hidden", ("mp", "width")),
            P(("mp", "width")),
        ),
        out_specs=(
            P("mp", "hidden", "width"),
            P(None, "hidden"),
            P(("mp", "width"), "hidden"),
            P("hidden", ("mp", "width")),
            P("hidden"),
            P(("mp", "width")),
        ),
        check_vma=False,
    )
```

profile of v0, /device:TPU:0, one launch (start us, length us, event | category | flops | bytes accessed | tf_op | source)
XLA Modules:
  0.0 549.1 jit_solution(14673929088239518730)
XLA Ops:
  7.2 0.0 all-gather.9.cloned.1.call-start
  7.2 0.7 all-gather.9.cloned.1.call-update
  7.9 0.0 reduce-scatter.4.cloned.1.call-start
  7.9 47.0 %all-gather.9.cloned.1.call-done = bf16[1,512,3584]{2,1,0:T(8,128)(2,1)} async-done(((bf16[1,64,3584]{2,1,0:T(8,128)(2,1)}), bf16[1,512,3584]{2,1,0:T(8,128)(2,1)}) %all-gather.9.cloned.1.call-update) | async-done | bytes 3670032 | tf_op jit(solution)/shard_map/all_gather | solution.py:18
  54.9 9.6 %fusion.4 = f32[512,896]{1,0:T(8,128)S(1)} fusion(bf16[1,896,3584]{2,1,0:T(8,128)(2,1)} %param.9, bf16[1,512,3584]{2,1,0:T(8,128)(2,1)} %all-gather.9.cloned.1.call-done), kind=kOutput, calls=%fused_computation.7 | convolution fusion | flops 3288334336 | bytes 11927552 | tf_op jit(solution)/shard_map/dot_general | solution.py:19
  64.5 0.0 copy-done.7
  64.6 0.0 slice-start.1
  64.6 7.1 %fusion.17 = bf16[512,896]{1,0:T(8,128)(2,1)S(1)} fusion(f32[512,896]{1,0:T(8,128)S(1)} %fusion.4, bf16[1,896,3584]{2,1,0:T(8,128)(2,1)} %param.10, bf16[1,512,3584]{2,1,0:T(8,128)(2,1)S(1)} %copy-done.7), kind=kOutput, calls=%fused_computation.25 | convolution fusion | flops 3292921856 | bytes 12845056 | tf_op jit(solution)/shard_map/dot_general | solution.py:22
  71.7 0.0 slice-done
  71.7 0.0 slice-done.1
  71.7 6.0 %fusion = f32[512,3584]{1,0:T(8,128)} fusion(bf16[512,896]{1,0:T(8,128)(2,1)S(1)} %fusion.17, bf16[1,896,3584]{2,1,0:T(8,128)(2,1)S(1)} %bitcast.36), kind=kOutput, calls=%fused_computation.3 | convolution fusion | flops 3288334336 | bytes 14680064 | tf_op jit(solution)/shard_map/dot_general | solution.py:26
  77.8 0.0 reduce-scatter.4.cloned.1.call-update
  77.8 0.0 reduce-scatter.6.cloned.1.call-start
  77.9 78.6 %reduce-scatter.4.cloned.1.call-done = f32[64,3584]{1,0:T(8,128)} async-done(((f32[512,3584]{1,0:T(8,128)}), f32[64,3584]{1,0:T(8,128)}) %reduce-scatter.4.cloned.1.call-update) | async-done | bytes 917520 | tf_op jit(solution)/shard_map/reduce_scatter | solution.py:25
  156.4 0.0 reduce-scatter.6.cloned.1.call-update
  156.4 0.0 all-gather.5.cloned.1.call-start
  156.5 19.6 %reduce-scatter.6.cloned.1.call-done = f32[64,1792]{1,0:T(8,128)} async-done(((f32[64,3584]{1,0:T(8,128)}), f32[64,1792]{1,0:T(8,128)}) %reduce-scatter.6.cloned.1.call-update) | async-done | bytes 458768 | tf_op jit(solution)/shard_map/reduce_scatter | solution.py:31
  176.1 1.7 convert_element_type.23
  177.8 0.0 all-gather.5.cloned.1.call-update
  177.9 0.3 all-reduce.3.cloned.1.call-start
  178.2 27.0 %all-gather.5.cloned.1.call-done = bf16[512,1792]{1,0:T(8,128)(2,1)} async-done(((bf16[64,1792]{1,0:T(8,128)(2,1)}), bf16[512,1792]{1,0:T(8,128)(2,1)}) %all-gather.5.cloned.1.call-update) | async-done | bytes 1835024 | tf_op jit(solution)/shard_map/all_gather | solution.py:33
  205.2 16.9 %fusion.26 = f32[512,2048]{1,0:T(8,128)} fusion(bf16[512,1792]{1,0:T(8,128)(2,1)} %all-gather.5.cloned.1.call-done, f32[1792,2048]{1,0:T(8,128)} %param.12), kind=kOutput, calls=%fused_computation.36 | convolution fusion | flops 22548578304 | bytes 20709376 | tf_op jit(solution)/shard_map/dot_general | solution.py:34
  222.1 0.0 all-reduce.3.cloned.1.call-update
  222.1 0.4 reduce-scatter.8.cloned.1.call-start
  222.5 102.8 %all-reduce.3.cloned.1.call-done = f32[512,2048]{1,0:T(8,128)} async-done(((f32[512,2048]{1,0:T(8,128)}), f32[512,2048]{1,0:T(8,128)}) %all-reduce.3.cloned.1.call-update) | async-done | bytes 4194320 | tf_op jit(solution)/shard_map/psum | solution.py:38
  325.3 4.9 fusion.24
  330.2 0.0 copy-start
  330.2 2.0 copy-done
  332.2 26.6 %fusion.27 = f32[512,1792]{1,0:T(8,128)} fusion(f32[512,2048]{1,0:T(8,128)S(1)} %get-tuple-element.7, f32[2048,1792]{1,0:T(8,128)} %param.14), kind=kOutput, calls=%fused_computation.37 | convolution fusion | flops 22548578304 | bytes 22544384 | tf_op jit(solution)/shard_map/dot_general | solution.py:42
  358.9 0.0 reduce-scatter.8.cloned.1.call-update
  358.9 0.0 all-gather.7.cloned.1.call-start
  359.0 45.1 %reduce-scatter.8.cloned.1.call-done = f32[64,1792]{1,0:T(8,128)} async-done(((f32[512,1792]{1,0:T(8,128)}), f32[64,1792]{1,0:T(8,128)}) %reduce-scatter.8.cloned.1.call-update) | async-done | bytes 458768 | tf_op jit(solution)/shard_map/reduce_scatter | solution.py:43
  404.0 0.0 copy-done.6
  404.1 1.8 multiply_convert_fusion
  405.8 0.0 all-gather.7.cloned.1.call-update
  405.8 0.0 all-reduce.5.cloned.1.call-start
  405.9 6.2 %multiply_reduce_fusion = f32[2048]{0:T(1024)S(1)} fusion(f32[2048,1792]{1,0:T(8,128)} %param.14), kind=kLoop, calls=%fused_computation.1 | loop fusion | flops 7337984 | bytes 14688256 | tf_op jit(solution)/shard_map/reduce_sum | solution.py:36
  412.1 0.1 broadcast_select_fusion
  412.2 16.5 %psum.23 = f32[2,2048]{1,0:T(2,128)S(1)} all-reduce(f32[2,2048]{1,0:T(2,128)S(1)} %broadcast_select_fusion), channel_id=1, replica_groups=mesh['mp'=2,'width'=2,'hidden'=8] {'mp','width'}, use_global_device_ids=true, to_apply=%region_6.7 | all-reduce | flops 4096 | bytes 32768 | tf_op jit(solution)/shard_map/psum | solution.py:38
  428.8 2.9 all-gather.7.cloned.1.call-done
  431.7 18.4 %convolution_convert_fusion = bf16[512,2048]{1,0:T(8,128)(2,1)} fusion(bf16[512,1792]{1,0:T(8,128)(2,1)} %all-gather.7.cloned.1.call-done, f32[2048,1792]{1,0:T(8,128)} %param.14), kind=kOutput, calls=%fused_computation.15 | convolution fusion | flops 22549626880 | bytes 18612224 | tf_op jit(solution)/shard_map/dot_general | solution.py:49
  450.1 0.0 all-reduce.5.cloned.1.call-update
  450.1 0.7 convert_bitcast_fusion
  450.8 0.9 convert_reduce_fusion
  451.7 19.6 %multiply_add_fusion = f32[2048,1792]{1,0:T(8,128)} fusion(f32[2048,1792]{1,0:T(8,128)} %param.14, f32[512,2048]{1,0:T(8,128)} %copy-done, bf16[512,1792]{1,0:T(8,128)(2,1)S(1)} %copy-done.2, f32[2048]{0:T(1024)S(1)} %divide_multiply_fusion.1), kind=kOutput, calls=%fused_computation | convolution fusion | flops 22555918336 | bytes 35397632 | tf_op jit(solution)/shard_map/dot_general | solution.py:62
  471.3 47.8 %all-reduce.5.cloned.1.call-done = bf16[512,2048]{1,0:T(8,128)(2,1)} async-done(((bf16[512,2048]{1,0:T(8,128)(2,1)}), bf16[512,2048]{1,0:T(8,128)(2,1)}) %all-reduce.5.cloned.1.call-update) | async-done | bytes 2097168 | tf_op jit(solution)/shard_map/psum | solution.py:52
  519.2 5.0 fusion.22
  524.1 17.9 %fusion.23 = f32[1792,2048]{1,0:T(8,128)} fusion(bf16[512,1792]{1,0:T(8,128)(2,1)} %all-gather.5.cloned.1.call-done, bf16[512,2048]{1,0:T(8,128)(2,1)S(1)} %copy-done.4, f32[512,2048]{1,0:T(8,128)S(1)} %copy-done.1, f32[2048]{0:T(1024)S(1)} %bitcast.33, f32[2048]{0:T(1024)S(1)} %copy-done.5), kind=kOutput, calls=%fused_computation.34 | convolution fusion | flops 22556966912 | bytes 22822912 | tf_op jit(solution)/shard_map/dot_general | solution.py:57
  (18 shorter events, 0.1 us)
Async XLA Ops:
  7.2 47.7 %all-gather.9.cloned.1.call-start = ((), (), s32[]{:S(2)}) async-start(), calls=%async_computation.10 | async-start | bytes 4128768 | tf_op jit(solution)/shard_map/all_gather | solution.py:18
  7.9 148.5 %reduce-scatter.4.cloned.1.call-start = ((), (), s32[]{:S(2)}) async-start(), calls=%async_computation.3 | async-start | bytes 8257536 | tf_op jit(solution)/shard_map/reduce_scatter | solution.py:25
  54.9 9.6 %copy-start.7 = (bf16[1,512,3584]{2,1,0:T(8,128)(2,1)S(1)}, bf16[1,512,3584]{2,1,0:T(8,128)(2,1)}, u32[]{:S(2)}) copy-start(bf16[1,512,3584]{2,1,0:T(8,128)(2,1)} %all-gather.9.cloned.1.call-done) | copy-start | bytes 11010052
  54.9 16.8 %slice-start = ((s8[6422528]{0:T(1024)(128)(4,1)}), s8[4194304]{0:T(1024)(128)(4,1)S(1)}, s32[]{:S(2)}) async-start(s8[6422528]{0:T(1024)(128)(4,1)} %bitcast.35), calls=%async_computation.11 | async-start | bytes 8388608
  64.6 7.2 %slice-start.1 = ((s8[6422528]{0:T(1024)(128)(4,1)}), s8[2228224]{0:T(1024)(128)(4,1)S(1)}, s32[]{:S(2)}) async-start(s8[6422528]{0:T(1024)(128)(4,1)} %bitcast.35), calls=%async_computation.12 | async-start | bytes 4456448
  77.8 98.3 %reduce-scatter.6.cloned.1.call-start = ((), (), s32[]{:S(2)}) async-start(), calls=%async_computation.4 | async-start | bytes 1376256 | tf_op jit(solution)/shard_map/reduce_scatter | solution.py:31
  156.4 48.8 %all-gather.5.cloned.1.call-start = ((), (), s32[]{:S(2)}) async-start(), calls=%async_computation.5 | async-start | bytes 2064384 | tf_op jit(solution)/shard_map/all_gather | solution.py:33
  177.9 147.4 %all-reduce.3.cloned.1.call-start = ((), (), s32[]{:S(2)}) async-start(), calls=%async_computation.6 | async-start | bytes 8388608 | tf_op jit(solution)/shard_map/psum | solution.py:38
  222.1 103.2 %copy-start.5 = (f32[2048]{0:T(1024)S(1)}, f32[2048]{0:T(1024)}, u32[]{:S(2)}) copy-start(f32[2048]{0:T(1024)} %param.13) | copy-start | bytes 24580
  222.1 181.9 %reduce-scatter.8.cloned.1.call-start = ((), (), s32[]{:S(2)}) async-start(), calls=%async_computation.7 | async-start | bytes 4128768 | tf_op jit(solution)/shard_map/reduce_scatter | solution.py:43
  330.2 2.0 copy-start
  332.2 71.8 %copy-start.3 = (f32[64,1792]{1,0:T(8,128)S(1)}, f32[64,1792]{1,0:T(8,128)}, u32[]{:S(2)}) copy-start(f32[64,1792]{1,0:T(8,128)} %reduce-scatter.6.cloned.1.call-done) | copy-start | bytes 1376260
  332.2 71.8 %copy-start.6 = (f32[1792]{0:T(1024)S(1)}, f32[1792]{0:T(1024)}, u32[]{:S(2)}) copy-start(f32[1792]{0:T(1024)} %param.15) | copy-start | bytes 21508
  358.9 72.7 %all-gather.7.cloned.1.call-start = ((), (), s32[]{:S(2)}) async-start(), calls=%async_computation.8 | async-start | bytes 2064384 | tf_op jit(solution)/shard_map/all_gather | solution.py:45
  405.8 113.3 %all-reduce.5.cloned.1.call-start = ((), (), s32[]{:S(2)}) async-start(), calls=%async_computation.9 | async-start | bytes 4194304 | tf_op jit(solution)/shard_map/psum | solution.py:52
  431.7 19.2 %copy-start.2 = (bf16[512,1792]{1,0:T(8,128)(2,1)S(1)}, bf16[512,1792]{1,0:T(8,128)(2,1)}, u32[]{:S(2)}) copy-start(bf16[512,1792]{1,0:T(8,128)(2,1)} %all-gather.7.cloned.1.call-done) | copy-start | bytes 5505028
  519.1 5.0 copy-start.1
  519.1 5.0 copy-start.4
Sparse Core Ops, SparseCore 0:
  9.6 45.2 all-gather.8
  77.9 78.4 reduce-scatter.3
  158.7 17.3 reduce-scatter.5
  178.2 26.9 all-gather.4
  222.2 103.0 all-reduce.2
  359.0 44.9 reduce-scatter.7
  406.3 25.3 all-gather.6
  450.2 68.8 all-reduce.4
where the time goes:
time: 555 us; the launch traced here: 549 us
  waiting for transfers between devices  372 us (67%)
  matrix products  122 us (22%)
  other arithmetic  21.3 us (4%)
  blocking collectives  16.5 us (3%)
  between operations  14.5 us (3%)
    psum x1, waiting for transfers between devices, body(): pre_sum, square_sums = lax.psum((enc_partial, square_pair), ('mp', 'width'))  103 us
    reduce_scatter x1, waiting for transfers between devices, body(): lax.psum_scatter(jnp.dot(hidden_act, down_local, preferred_element_type=j...  78.6 us
    psum x1, waiting for transfers between devices, body(): lax.psum(back_part.astype(jnp.bfloat16), ('mp', 'width'))  47.8 us
    all_gather x1, waiting for transfers between devices, body(): gathered = lax.all_gather(residual_in[0], 'hidden', axis=0, tiled=True)  47 us
    reduce_scatter x1, waiting for transfers between devices, body(): lax.psum_scatter(recon_part, 'hidden', scatter_dimension=0, tiled=True)  45.1 us
    all_gather x1, waiting for transfers between devices, body(): lax.all_gather(mlp_acts, 'hidden', axis=0, tiled=True).astype(jnp.float32)  27 us
    dot_general x1, matrix products, body(): recon_part = jnp.dot(latents, dec_weight, precision=highest)  26.6 us
    reduce_scatter x1, waiting for transfers between devices, body(): lax.psum_scatter(row_sums, 'width', scatter_dimension=1, tiled=True)  19.6 us
  transfers between devices with their start and end apart: 8, of which 8 were waited for; matrix products, arithmetic and copies ran while one was open for 5% of the time, Pallas kernels for 0%

commit v1 on v0

--- a/solution.py
+++ b/solution.py
@@ -8,6 +8,7 @@
 sparsity_coef = 0.02
 norm_floor = 1e-06
 highest = lax.Precision.HIGHEST
+advance_positions = lambda x_in: lax.psum(lax.psum(x_in, "mp"), "width")
 
 
 def body(
@@ -35,7 +36,7 @@
     model_index = lax.axis_index("mp")
     squares = jnp.sum(dec_weight * dec_weight, axis=1)
     square_pair = jnp.where(jnp.arange(2)[:, None] == model_index, squares[None, :], 0.0)
-    pre_sum, square_sums = lax.psum((enc_partial, square_pair), ("mp", "width"))
+    pre_sum, square_sums = advance_positions((enc_partial, square_pair))
     pre_act = pre_sum + enc_bias
     latents = jax.nn.softplus(sharpness * pre_act) / sharpness
     dec_norms = jnp.sqrt(square_sums + norm_floor)

time: 555 us -> 669 us (1.21)
  waiting for transfers between devices: 372 us -> 486 us
    psum x1 -> x2, waiting for transfers between devices: 103 us -> 217 us  [advance_positions = lambda x_in: lax.psum(lax.psum(x_in, 'mp'), 'width')]
    psum x1 -> x2, blocking collectives: 16.5 us -> 16.8 us  [advance_positions = lambda x_in: lax.psum(lax.psum(x_in, 'mp'), 'width')]
  transfers between devices with their start and end apart: 8 -> 9, of which waited for: 8 -> 9; matrix products, arithmetic and copies ran while one was open for 5% -> 4% of each run, Pallas kernels for 0% -> 0%
where the time goes in v1:
time: 669 us; the launch traced here: 663 us
  waiting for transfers between devices  486 us (73%)
  matrix products  122 us (18%)
  other arithmetic  21.3 us (3%)
  blocking collectives  16.8 us (3%)
  between operations  14.2 us (2%)
    psum x2, waiting for transfers between devices, advance_positions = lambda x_in: lax.psum(lax.psum(x_in, 'mp'), 'width')  217 us
    reduce_scatter x1, waiting for transfers between devices, body(): lax.psum_scatter(jnp.dot(hidden_act, down_local, preferred_element_type=j...  78.6 us
    psum x1, waiting for transfers between devices, body(): lax.psum(back_part.astype(jnp.bfloat16), ('mp', 'width'))  47.9 us
    all_gather x1, waiting for transfers between devices, body(): gathered = lax.all_gather(residual_in[0], 'hidden', axis=0, tiled=True)  47 us
    reduce_scatter x1, waiting for transfers between devices, body(): lax.psum_scatter(recon_part, 'hidden', scatter_dimension=0, tiled=True)  45.1 us
    all_gather x1, waiting for transfers between devices, body(): lax.all_gather(mlp_acts, 'hidden', axis=0, tiled=True).astype(jnp.float32)  27 us
    dot_general x1, matrix products, body(): recon_part = jnp.dot(latents, dec_weight, precision=highest)  26.6 us
    reduce_scatter x1, waiting for transfers between devices, body(): lax.psum_scatter(row_sums, 'width', scatter_dimension=1, tiled=True)  19.6 us
  transfers between devices with their start and end apart: 9, of which 9 were waited for; matrix products, arithmetic and copies ran while one was open for 4% of the time, Pallas kernels for 0%

profile of v1, /device:TPU:0, one launch (start us, length us, event | category | flops | bytes accessed | tf_op | source)
XLA Modules:
  0.0 663.3 jit_solution(14955147231079574819)
XLA Ops:
  7.2 0.0 all-gather.9.cloned.1.call-start
  7.2 0.7 all-gather.9.cloned.1.call-update
  7.9 0.0 reduce-scatter.4.cloned.1.call-start
  7.9 47.0 %all-gather.9.cloned.1.call-done = bf16[1,512,3584]{2,1,0:T(8,128)(2,1)} async-done(((bf16[1,64,3584]{2,1,0:T(8,128)(2,1)}), bf16[1,512,3584]{2,1,0:T(8,128)(2,1)}) %all-gather.9.cloned.1.call-update) | async-done | bytes 3670032 | tf_op jit(solution)/shard_map/all_gather | solution.py:19
  54.9 9.6 %fusion.4 = f32[512,896]{1,0:T(8,128)S(1)} fusion(bf16[1,896,3584]{2,1,0:T(8,128)(2,1)} %param.9, bf16[1,512,3584]{2,1,0:T(8,128)(2,1)} %all-gather.9.cloned.1.call-done), kind=kOutput, calls=%fused_computation.7 | convolution fusion | flops 3288334336 | bytes 11927552 | tf_op jit(solution)/shard_map/dot_general | solution.py:20
  64.6 0.0 slice-start.1
  64.6 7.1 %fusion.17 = bf16[512,896]{1,0:T(8,128)(2,1)S(1)} fusion(f32[512,896]{1,0:T(8,128)S(1)} %fusion.4, bf16[1,896,3584]{2,1,0:T(8,128)(2,1)} %param.10, bf16[1,512,3584]{2,1,0:T(8,128)(2,1)S(1)} %copy-done.7), kind=kOutput, calls=%fused_computation.25 | convolution fusion | flops 3292921856 | bytes 12845056 | tf_op jit(solution)/shard_map/dot_general | solution.py:23
  71.7 6.0 fusion
  77.8 0.0 reduce-scatter.4.cloned.1.call-update
  77.8 0.0 reduce-scatter.6.cloned.1.call-start
  77.9 78.6 %reduce-scatter.4.cloned.1.call-done = f32[64,3584]{1,0:T(8,128)} async-done(((f32[512,3584]{1,0:T(8,128)}), f32[64,3584]{1,0:T(8,128)}) %reduce-scatter.4.cloned.1.call-update) | async-done | bytes 917520 | tf_op jit(solution)/shard_map/reduce_scatter | solution.py:26
  156.4 0.0 reduce-scatter.6.cloned.1.call-update
  156.4 0.0 all-gather.5.cloned.1.call-start
  156.5 19.6 %reduce-scatter.6.cloned.1.call-done = f32[64,1792]{1,0:T(8,128)} async-done(((f32[64,3584]{1,0:T(8,128)}), f32[64,1792]{1,0:T(8,128)}) %reduce-scatter.6.cloned.1.call-update) | async-done | bytes 458768 | tf_op jit(solution)/shard_map/reduce_scatter | solution.py:32
  176.1 1.7 convert_element_type.23
  177.8 0.0 all-gather.5.cloned.1.call-update
  177.9 0.3 all-reduce.4.cloned.1.call-start
  178.2 27.0 %all-gather.5.cloned.1.call-done = bf16[512,1792]{1,0:T(8,128)(2,1)} async-done(((bf16[64,1792]{1,0:T(8,128)(2,1)}), bf16[512,1792]{1,0:T(8,128)(2,1)}) %all-gather.5.cloned.1.call-update) | async-done | bytes 1835024 | tf_op jit(solution)/shard_map/all_gather | solution.py:34
  205.2 16.9 %fusion.26 = f32[512,2048]{1,0:T(8,128)} fusion(bf16[512,1792]{1,0:T(8,128)(2,1)} %all-gather.5.cloned.1.call-done, f32[1792,2048]{1,0:T(8,128)} %param.12), kind=kOutput, calls=%fused_computation.36 | convolution fusion | flops 22548578304 | bytes 20709376 | tf_op jit(solution)/shard_map/dot_general | solution.py:35
  222.1 0.0 all-reduce.4.cloned.1.call-update
  222.1 0.0 all-reduce.6.cloned.1.call-start
  222.2 107.4 %all-reduce.4.cloned.1.call-done = f32[512,2048]{1,0:T(8,128)} async-done(((f32[512,2048]{1,0:T(8,128)}), f32[512,2048]{1,0:T(8,128)}) %all-reduce.4.cloned.1.call-update) | async-done | bytes 4194320 | tf_op jit(solution)/shard_map/psum | solution.py:11
  329.6 0.0 all-reduce.6.cloned.1.call-update
  329.6 0.4 reduce-scatter.8.cloned.1.call-start
  330.0 109.9 %all-reduce.6.cloned.1.call-done = f32[512,2048]{1,0:T(8,128)} async-done(((f32[512,2048]{1,0:T(8,128)}), f32[512,2048]{1,0:T(8,128)}) %all-reduce.6.cloned.1.call-update) | async-done | bytes 4194320 | tf_op jit(solution)/shard_map/psum | solution.py:11
  439.9 4.9 fusion.24
  444.8 0.0 copy-start
  444.8 2.0 copy-done
  446.8 26.6 %fusion.27 = f32[512,1792]{1,0:T(8,128)} fusion(f32[512,2048]{1,0:T(8,128)S(1)} %get-tuple-element.7, f32[2048,1792]{1,0:T(8,128)} %param.14), kind=kOutput, calls=%fused_computation.37 | convolution fusion | flops 22548578304 | bytes 22544384 | tf_op jit(solution)/shard_map/dot_general | solution.py:43
  473.4 0.0 reduce-scatter.8.cloned.1.call-update
  473.5 0.0 all-gather.7.cloned.1.call-start
  473.5 45.1 %reduce-scatter.8.cloned.1.call-done = f32[64,1792]{1,0:T(8,128)} async-done(((f32[512,1792]{1,0:T(8,128)}), f32[64,1792]{1,0:T(8,128)}) %reduce-scatter.8.cloned.1.call-update) | async-done | bytes 458768 | tf_op jit(solution)/shard_map/reduce_scatter | solution.py:44
  518.6 1.8 multiply_convert_fusion
  520.3 0.0 all-gather.7.cloned.1.call-update
  520.4 0.0 all-reduce.8.cloned.1.call-start
  520.4 6.2 multiply_reduce_fusion
  526.6 0.1 broadcast_select_fusion
  526.7 8.1 %psum.38 = f32[2,2048]{1,0:T(2,128)S(1)} all-reduce(f32[2,2048]{1,0:T(2,128)S(1)} %broadcast_select_fusion), channel_id=1, replica_groups=mesh['mp'=2,'width'=2,'hidden'=8] {'mp'}, use_global_device_ids=true, to_apply=%region_7.8 | all-reduce | flops 4096 | bytes 32768 | tf_op jit(solution)/shard_map/psum | solution.py:11
  534.9 8.7 %psum.39 = f32[2,2048]{1,0:T(2,128)S(1)} all-reduce(f32[2,2048]{1,0:T(2,128)S(1)} %psum.38), channel_id=1, replica_groups=mesh['mp'=2,'width'=2,'hidden'=8] {'width'}, use_global_device_ids=true, to_apply=%region_8.9 | all-reduce | flops 4096 | bytes 32768 | tf_op jit(solution)/shard_map/psum | solution.py:11
  543.6 2.6 all-gather.7.cloned.1.call-done
  546.2 18.4 %convolution_convert_fusion = bf16[512,2048]{1,0:T(8,128)(2,1)} fusion(bf16[512,1792]{1,0:T(8,128)(2,1)} %all-gather.7.cloned.1.call-done, f32[2048,1792]{1,0:T(8,128)} %param.14), kind=kOutput, calls=%fused_computation.15 | convolution fusion | flops 22549626880 | bytes 18612224 | tf_op jit(solution)/shard_map/dot_general | solution.py:50
  564.6 0.0 all-reduce.8.cloned.1.call-update
  564.6 0.7 convert_bitcast_fusion
  565.3 0.9 convert_reduce_fusion
  566.2 19.6 %multiply_add_fusion = f32[2048,1792]{1,0:T(8,128)} fusion(f32[2048,1792]{1,0:T(8,128)} %param.14, f32[512,2048]{1,0:T(8,128)} %copy-done, bf16[512,1792]{1,0:T(8,128)(2,1)S(1)} %copy-done.2, f32[2048]{0:T(1024)S(1)} %divide_multiply_fusion.1), kind=kOutput, calls=%fused_computation | convolution fusion | flops 22555918336 | bytes 35397632 | tf_op jit(solution)/shard_map/dot_general | solution.py:63
  585.8 47.9 %all-reduce.8.cloned.1.call-done = bf16[512,2048]{1,0:T(8,128)(2,1)} async-done(((bf16[512,2048]{1,0:T(8,128)(2,1)}), bf16[512,2048]{1,0:T(8,128)(2,1)}) %all-reduce.8.cloned.1.call-update) | async-done | bytes 2097168 | tf_op jit(solution)/shard_map/psum | solution.py:53
  633.7 5.0 fusion.22
  638.6 17.9 %fusion.23 = f32[1792,2048]{1,0:T(8,128)} fusion(bf16[512,1792]{1,0:T(8,128)(2,1)} %all-gather.5.cloned.1.call-done, bf16[512,2048]{1,0:T(8,128)(2,1)S(1)} %copy-done.4, f32[512,2048]{1,0:T(8,128)S(1)} %copy-done.1, f32[2048]{0:T(1024)S(1)} %bitcast.33, f32[2048]{0:T(1024)S(1)} %copy-done.5), kind=kOutput, calls=%fused_computation.34 | convolution fusion | flops 22556966912 | bytes 22822912 | tf_op jit(solution)/shard_map/dot_general | solution.py:58
  (22 shorter events, 0.1 us)
Async XLA Ops:
  7.2 47.7 %all-gather.9.cloned.1.call-start = ((), (), s32[]{:S(2)}) async-start(), calls=%async_computation.11 | async-start | bytes 4128768 | tf_op jit(solution)/shard_map/all_gather | solution.py:19
  7.9 148.5 %reduce-scatter.4.cloned.1.call-start = ((), (), s32[]{:S(2)}) async-start(), calls=%async_computation.3 | async-start | bytes 8257536 | tf_op jit(solution)/shard_map/reduce_scatter | solution.py:26
  54.9 9.6 %copy-start.7 = (bf16[1,512,3584]{2,1,0:T(8,128)(2,1)S(1)}, bf16[1,512,3584]{2,1,0:T(8,128)(2,1)}, u32[]{:S(2)}) copy-start(bf16[1,512,3584]{2,1,0:T(8,128)(2,1)} %all-gather.9.cloned.1.call-done) | copy-start | bytes 11010052
  54.9 16.8 %slice-start = ((s8[6422528]{0:T(1024)(128)(4,1)}), s8[4194304]{0:T(1024)(128)(4,1)S(1)}, s32[]{:S(2)}) async-start(s8[6422528]{0:T(1024)(128)(4,1)} %bitcast.35), calls=%async_computation.12 | async-start | bytes 8388608
  64.6 7.2 %slice-start.1 = ((s8[6422528]{0:T(1024)(128)(4,1)}), s8[2228224]{0:T(1024)(128)(4,1)S(1)}, s32[]{:S(2)}) async-start(s8[6422528]{0:T(1024)(128)(4,1)} %bitcast.35), calls=%async_computation.13 | async-start | bytes 4456448
  77.8 98.3 %reduce-scatter.6.cloned.1.call-start = ((), (), s32[]{:S(2)}) async-start(), calls=%async_computation.4 | async-start | bytes 1376256 | tf_op jit(solution)/shard_map/reduce_scatter | solution.py:32
  156.4 48.8 %all-gather.5.cloned.1.call-start = ((), (), s32[]{:S(2)}) async-start(), calls=%async_computation.5 | async-start | bytes 2064384 | tf_op jit(solution)/shard_map/all_gather | solution.py:34
  177.9 151.7 %all-reduce.4.cloned.1.call-start = ((), (), s32[]{:S(2)}) async-start(), calls=%async_computation.6 | async-start | bytes 8388608 | tf_op jit(solution)/shard_map/psum | solution.py:11
  222.1 217.8 %copy-start.5 = (f32[2048]{0:T(1024)S(1)}, f32[2048]{0:T(1024)}, u32[]{:S(2)}) copy-start(f32[2048]{0:T(1024)} %param.13) | copy-start | bytes 24580
  222.1 217.8 %all-reduce.6.cloned.1.call-start = ((), (), s32[]{:S(2)}) async-start(), calls=%async_computation.7 | async-start | bytes 8388608 | tf_op jit(solution)/shard_map/psum | solution.py:11
  329.6 188.9 %reduce-scatter.8.cloned.1.call-start = ((), (), s32[]{:S(2)}) async-start(), calls=%async_computation.8 | async-start | bytes 4128768 | tf_op jit(solution)/shard_map/reduce_scatter | solution.py:44
  444.8 2.0 copy-start
  446.8 71.8 %copy-start.3 = (f32[64,1792]{1,0:T(8,128)S(1)}, f32[64,1792]{1,0:T(8,128)}, u32[]{:S(2)}) copy-start(f32[64,1792]{1,0:T(8,128)} %reduce-scatter.6.cloned.1.call-done) | copy-start | bytes 1376260
  446.8 71.8 %copy-start.6 = (f32[1792]{0:T(1024)S(1)}, f32[1792]{0:T(1024)}, u32[]{:S(2)}) copy-start(f32[1792]{0:T(1024)} %param.15) | copy-start | bytes 21508
  473.5 72.7 %all-gather.7.cloned.1.call-start = ((), (), s32[]{:S(2)}) async-start(), calls=%async_computation.9 | async-start | bytes 2064384 | tf_op jit(solution)/shard_map/all_gather | solution.py:46
  520.4 113.3 %all-reduce.8.cloned.1.call-start = ((), (), s32[]{:S(2)}) async-start(), calls=%async_computation.10 | async-start | bytes 4194304 | tf_op jit(solution)/shard_map/psum | solution.py:53
  546.2 19.1 %copy-start.2 = (bf16[512,1792]{1,0:T(8,128)(2,1)S(1)}, bf16[512,1792]{1,0:T(8,128)(2,1)}, u32[]{:S(2)}) copy-start(bf16[512,1792]{1,0:T(8,128)(2,1)} %all-gather.7.cloned.1.call-done) | copy-start | bytes 5505028
  633.7 5.0 copy-start.1
  633.7 5.0 copy-start.4
Sparse Core Ops, SparseCore 0:
  9.6 45.2 all-gather.8
  77.9 78.4 reduce-scatter.3
  158.7 17.3 reduce-scatter.5
  178.2 26.9 all-gather.4
  222.2 107.3 all-reduce.3
  331.9 107.9 all-reduce.5
  473.6 44.9 reduce-scatter.7
  520.8 25.3 all-gather.6
  564.7 68.8 all-reduce.7
